TPU v7x, 32 devices: a whole 2x2x4 slice. The times are simulated.
32 devices in a mesh: tm: 8 (over z, x), clip: 4 (over y, core).
Axes of the slice: x: 2, y: 2, z: 4, core: 2. Of those that a mesh axis runs over, the one named last changes fastest.
Arguments:
- video: float32 [4, 8, 16, 32, 320], P('clip', 'tm'), may hold values from -6 to 6
- spatial_w: bfloat16 [9, 320, 320], P(None, 'clip'), may hold values from -0.109375 to 0.109375
- spatial_b: float32 [320], replicated, may hold values from -3 to 3
- temporal_w: float32 [3, 320, 320], P(None, 'clip'), may hold values from -0.1875 to 0.1875
- cotangent: float32 [4, 8, 16, 32, 320], P('clip', 'tm'), may hold values from -6 to 6
Outputs:
- output: float32 [4, 8, 16, 32, 320], P('clip', 'tm')
- grad_video: float32 [4, 8, 16, 32, 320], P('clip', 'tm')
- grad_temporal: float32 [3, 320, 320], P(None, 'clip')
All inputs are finite; a program needn't handle non-finite values.
Results may differ from a plain program's by a relative error of at most 0.0049.
Values may be sent and summed in bfloat16 or wider, within the bound.
A program may use at most 64 MiB of HBM per device.

v0:
```python
import math
import jax
import jax.numpy as jnp
from jax import lax
from jax.sharding import PartitionSpec as P


def padded_2(cells, sides, width):
    for axis, dim in sides:
        count = lax.axis_size(axis)
        ends = count - 1
        head = lax.slice_in_dim(cells, 0, width, axis=dim)
        tail = lax.slice_in_dim(cells, cells.shape[dim] - width, cells.shape[dim], axis=dim)
        cells = jnp.concatenate(
            [
                lax.ppermute(tail, axis, [(i, (i + 1) % count) for i in range(ends)]),
                cells,
                lax.ppermute(head, axis, [((i + 1) % count, i) for i in range(ends)]),
            ],
            axis=dim,
        )
    return cells


def outer_dot(left, right):
    return lax.dot_general(
        left, right, (((0,), (0,)), ((), ())), preferred_element_type=jnp.float32
    )


def transpose_dot(left, right):
    return lax.dot_general(
        left, right, (((1,), (1,)), ((), ())), preferred_element_type=jnp.float32
    )


def on_device(video, spatial_w, spatial_b, temporal_w, cotangent):
    clips, frames, height, width, chans = video.shape
    row_count = clips * frames * height * width
    video_b = video.astype(jnp.bfloat16)
    padded = jnp.pad(video_b, ((0, 0), (0, 0), (1, 1), (1, 1), (0, 0)))
    temporal_b = temporal_w.astype(jnp.bfloat16)
    spatial_all, temporal_all = (
        lax.all_gather(spatial_w, "clip", axis=1, tiled=True),
        lax.all_gather(temporal_b, "clip", axis=1, tiled=True),
    )
    spatial = jnp.zeros((row_count, chans), jnp.float32)
    for shift_y in range(3):
        for shift_x in range(3):
            window = padded[:, :, shift_y : shift_y + height, shift_x : shift_x + width, :].reshape(
                row_count, chans
            )
            spatial = spatial + jnp.dot(
                window, spatial_all[3 * shift_y + shift_x], preferred_element_type=jnp.float32
            )
    spatial = spatial + spatial_b
    sigmoid_s = jax.nn.sigmoid(spatial)
    hidden = (spatial * sigmoid_s).astype(jnp.bfloat16).reshape(clips, frames, height, width, chans)
    hidden_pad = padded_2(hidden, (("tm", 1),), 1)
    temporal = jnp.zeros((row_count, chans), jnp.float32)
    for kernel_tap in range(3):
        shifted = hidden_pad[:, kernel_tap : kernel_tap + frames].reshape(row_count, chans)
        temporal = temporal + jnp.dot(
            shifted, temporal_all[kernel_tap], preferred_element_type=jnp.float32
        )
    output = video + temporal.reshape(video.shape)
    cot_b = cotangent.astype(jnp.bfloat16)
    cot_flat = cot_b.reshape(row_count, chans)
    cot_pad = padded_2(cot_b, (("tm", 1),), 1)
    grad_hidden = jnp.zeros((row_count, chans), jnp.float32)
    grads = []
    for kernel_tap in range(3):
        shifted_cot = cot_pad[:, 2 - kernel_tap : 2 - kernel_tap + frames].reshape(row_count, chans)
        grad_hidden = grad_hidden + transpose_dot(shifted_cot, temporal_all[kernel_tap])
        shifted_hid = hidden_pad[:, kernel_tap : kernel_tap + frames].reshape(row_count, chans)
        grads.append(outer_dot(shifted_hid, cot_flat))
    local_grad = jnp.stack(grads)
    total_rows = row_count * lax.axis_size("tm") * lax.axis_size("clip")
    summed = lax.psum(local_grad, "tm")
    owned = lax.psum_scatter(summed, "clip", scatter_dimension=1, tiled=True)
    grad_temporal = owned * (1.0 / math.sqrt(total_rows))
    grad_spatial = (grad_hidden * sigmoid_s * (1.0 + spatial * (1.0 - sigmoid_s))).astype(
        jnp.bfloat16
    )
    grad_frames = jnp.pad(
        grad_spatial.reshape(clips, frames, height, width, chans),
        ((0, 0), (0, 0), (1, 1), (1, 1), (0, 0)),
    )
    grad_acc = cotangent.reshape(row_count, chans)
    for shift_y in range(3):
        for shift_x in range(3):
            window = grad_frames[
                :, :, 2 - shift_y : 2 - shift_y + height, 2 - shift_x : 2 - shift_x + width, :
            ].reshape(row_count, chans)
            grad_acc = grad_acc + transpose_dot(window, spatial_all[3 * shift_y + shift_x])
    grad_video = grad_acc.reshape(video.shape)
    return (output, grad_video, grad_temporal)


def solution(mesh):
    return jax.shard_map(
        on_device,
        mesh=mesh,
        in_specs=(
            P("clip", "tm", None, None, None),
            P(None, "clip", None),
            P(),
            P(None, "clip", None),
            P("clip", "tm", None, None, None),
        ),
        out_specs=(
            P("clip", "tm", None, None, None),
            P("clip", "tm", None, None, None),
            P(None, "clip", None),
        ),
        check_vma=False,
    )
```

profile of v0, /device:TPU:0, one launch (start us, length us, event | category | flops | bytes accessed | tf_op | source)
XLA Modules:
  0.0 184.8 jit_solution(11059689400053077663)
XLA Ops:
  9.2 4.9 %collective-permute-start.3 = (bf16[1,1,16,32,320]{4,3,2,1,0:T(8,128)(2,1)S(1)}, bf16[1,1,16,32,320]{4,3,2,1,0:T(8,128)(2,1)S(1)}, u32[]{:S(2)}, u32[]{:S(2)}) collective-permute-start(bf16[1,1,16,32,320]{4,3,2,1,0:T(8,128)(2,1)S(1)} %convert_element_type.21), channel_id=1, source_target_pairs={{0,4},{4,8},{8,12},{12,16},{16,20},{20,24},{24,28},{1,5},{5,9},{9,... | collective-permute-start | bytes 983048 | tf_op jit(solution)/shard_map/ppermute | solution.py:16
  14.1 1.3 collective-permute-start.2
  15.5 10.1 %all_gather.7 = bf16[3,320,320]{2,1,0:T(8,128)(2,1)S(1)} all-gather(bf16[3,80,320]{2,1,0:T(8,128)(2,1)S(1)} %convert_element_type.20), channel_id=1, replica_groups=mesh['tm'=8,'clip'=4] {'clip'}, dimensions={1}, use_global_device_ids=true | all-gather | bytes 768000 | tf_op jit(solution)/shard_map/all_gather | solution.py:45
  25.6 1.8 pad_slice_fusion.8
  28.5 1.2 fusion.19
  30.8 1.2 fusion.21
  32.0 4.5 %all-gather.2.cloned.1.call-done = bf16[9,320,320]{2,1,0:T(8,128)(2,1)} async-done(((bf16[9,80,320]{2,1,0:T(8,128)(2,1)}), bf16[9,320,320]{2,1,0:T(8,128)(2,1)}) %all-gather.2.cloned.1.call-update) | async-done | bytes 1843216 | tf_op jit(solution)/shard_map/all_gather | solution.py:44
  36.5 1.6 fusion.14
  38.1 1.5 convolution_add_fusion.14
  39.6 1.4 convolution_add_fusion.13
  43.4 1.4 multiply_convert_fusion
  44.8 1.9 %copy.13 = bf16[512,320]{1,0:T(8,128)(2,1)} copy(bf16[512,320]{0,1:T(8,128)(2,1)} %get-tuple-element.22) | data formatting | bytes 655360 | tf_op jit(solution)/shard_map/convert_element_type | solution.py:58
  46.7 1.3 collective-permute-start.1
  48.0 5.9 %collective-permute-start = (bf16[1,1,16,32,320]{4,3,2,1,0:T(8,128)(2,1)}, bf16[1,1,16,32,320]{4,3,2,1,0:T(8,128)(2,1)}, u32[]{:S(2)}, u32[]{:S(2)}) collective-permute-start(bf16[1,1,16,32,320]{4,3,2,1,0:T(8,128)(2,1)} %bitcast.146), channel_id=1, source_target_pairs={{0,4},{4,8},{8,12},{12,16},{16,20},{20,24},{24,28},{1,5},{5,9},{9,... | collective-permute-start | bytes 983048 | tf_op jit(solution)/shard_map/ppermute | solution.py:16
  53.9 2.8 %fusion.9 = bf16[512,320]{0,1:T(8,128)(2,1)} fusion(f32[512,320]{0,1:T(8,128)} %fusion.21, f32[512,320]{0,1:T(8,128)} %fusion.19, bf16[512,320]{1,0:T(8,128)(2,1)} %bitcast.26, f32[512,320]{0,1:T(8,128)} %get-tuple-element.23, bf16[3,320,320]{2,1,0:T(8,128)(2,1)S(1)} %all_gather.7), kind=kOutput, calls=%fused_computation.25 | convolution fusion | flops 106659840 | bytes 2867200 | tf_op jit(solution)/shard_map/dot_general | solution.py:32
  56.7 1.9 %copy.15 = bf16[512,320]{1,0:T(8,128)(2,1)} copy(bf16[512,320]{0,1:T(8,128)(2,1)} %fusion.9) | data formatting | bytes 655360 | tf_op jit(solution)/shard_map/convert_element_type | solution.py:82
  58.6 4.4 %pad_slice_fusion.4 = (bf16[1,1,16,32,320]{4,3,2,1,0:T(8,128)(2,1)}, bf16[1,1,16,32,320]{4,3,2,1,0:T(8,128)(2,1)}, bf16[1,1,16,32,320]{4,3,2,1,0:T(8,128)(2,1)},...) fusion(bf16[1,1,16,32,320]{4,3,2,1,0:T(8,128)(2,1)} %bitcast.132), kind=kLoop, calls=%fused_computation.35 | loop fusion | bytes 2949120 | tf_op jit(solution)/shard_map/slice | solution.py:92
  63.0 1.2 fusion.15
  64.6 1.4 convolution_bitcast_fusion
  66.0 3.7 %collective-permute-done = bf16[1,1,16,32,320]{4,3,2,1,0:T(8,128)(2,1)} collective-permute-done((bf16[1,1,16,32,320]{4,3,2,1,0:T(8,128)(2,1)}, bf16[1,1,16,32,320]{4,3,2,1,0:T(8,128)(2,1)}, u32[]{:S(2)}, u32[]{:S(2)}) %collective-permute-start) | collective-permute-done | bytes 327712 | tf_op jit(solution)/shard_map/ppermute | solution.py:16
  69.6 1.3 convolution_bitcast_fusion.2
  71.0 1.2 pad_maximum_fusion
  72.3 1.4 fusion.16
  73.8 1.4 fusion.17
  77.6 1.2 fusion.3
  78.9 2.3 %copy.17 = f32[512,320]{1,0:T(8,128)} copy(f32[512,320]{0,1:T(8,128)} %fusion.3) | data formatting | bytes 1310720 | tf_op jit(solution)/shard_map/add | solution.py:95
  81.5 20.0 %reduce-scatter.2.cloned.1.call-done = f32[3,80,320]{2,1,0:T(8,128)} async-done(((f32[3,320,320]{2,1,0:T(8,128)}), f32[3,80,320]{2,1,0:T(8,128)}) %reduce-scatter.2.cloned.1.call-update) | async-done | bytes 307216 | tf_op jit(solution)/shard_map/reduce_scatter | solution.py:80
  101.6 1.4 fusion.22
  103.0 2.3 %fusion.7 = f32[512,320]{0,1:T(8,128)} fusion(f32[512,320]{0,1:T(8,128)S(1)} %fusion.22, f32[512,320]{0,1:T(8,128)S(1)} %fusion.20, bf16[512,320]{1,0:T(8,128)(2,1)} %bitcast.19, bf16[3,320,320]{2,1,0:T(8,128)(2,1)S(1)} %all_gather.7), kind=kOutput, calls=%fused_computation.15 | convolution fusion | flops 105185280 | bytes 2539520 | tf_op jit(solution)/shard_map/dot_general | solution.py:63
  105.2 1.3 copy.14
  107.6 69.0 %all-reduce.4.cloned.1.call-done = f32[3,80,320]{2,1,0:T(8,128)} async-done(((f32[3,80,320]{2,1,0:T(8,128)}), f32[3,80,320]{2,1,0:T(8,128)}) %all-reduce.4.cloned.1.call-update) | async-done | bytes 307216 | tf_op jit(solution)/shard_map/psum | solution.py:79
  176.5 1.7 broadcast_multiply_fusion
  (72 shorter events, 10.7 us)
Async XLA Ops:
  7.2 8.2 %copy-start.4 = (f32[1,1,16,32,320]{4,3,2,1,0:T(8,128)S(1)}, f32[1,1,16,32,320]{4,3,2,1,0:T(8,128)}, u32[]{:S(2)}) copy-start(f32[1,1,16,32,320]{4,3,2,1,0:T(8,128)} %param.5) | copy-start | bytes 1966084
  7.2 8.2 %copy-start.21 = (f32[3,80,320]{2,1,0:T(8,128)S(1)}, f32[3,80,320]{2,1,0:T(8,128)}, u32[]{:S(2)}) copy-start(f32[3,80,320]{2,1,0:T(8,128)} %param.8) | copy-start | bytes 921604
  7.2 29.3 %all-gather.2.cloned.1.call-start = ((), (), s32[]{:S(2)}) async-start(), calls=%async_computation.1 | async-start | bytes 2764800 | tf_op jit(solution)/shard_map/all_gather | solution.py:44
  7.9 93.6 %reduce-scatter.2.cloned.1.call-start = ((), (), s32[]{:S(2)}) async-start(), calls=%async_computation.2 | async-start | bytes 1843200 | tf_op jit(solution)/shard_map/reduce_scatter | solution.py:80
  9.2 21.7 %collective-permute-start.3 = (bf16[1,1,16,32,320]{4,3,2,1,0:T(8,128)(2,1)S(1)}, bf16[1,1,16,32,320]{4,3,2,1,0:T(8,128)(2,1)S(1)}, u32[]{:S(2)}, u32[]{:S(2)}) collective-permute-start(bf16[1,1,16,32,320]{4,3,2,1,0:T(8,128)(2,1)S(1)} %convert_element_type.21), channel_id=1, source_target_pairs={{0,4},{4,8},{8,12},{12,16},{16,20},{20,24},{24,28},{1,5},{5,9},{9,... | collective-permute-start | bytes 983048 | tf_op jit(solution)/shard_map/ppermute | solution.py:16
  14.1 39.9 %collective-permute-start.2 = (bf16[1,1,16,32,320]{4,3,2,1,0:T(8,128)(2,1)S(1)}, bf16[1,1,16,32,320]{4,3,2,1,0:T(8,128)(2,1)}, u32[]{:S(2)}, u32[]{:S(2)}) collective-permute-start(bf16[1,1,16,32,320]{4,3,2,1,0:T(8,128)(2,1)S(1)} %convert_element_type.21), channel_id=1, source_target_pairs={{4,0},{8,4},{12,8},{16,12},{20,16},{24,20},{28,24},{5,1},{9,5},{13... | collective-permute-start | bytes 983048 | tf_op jit(solution)/shard_map/ppermute | solution.py:18
  15.4 11.9 %copy-start.1 = (bf16[1,1,16,32,320]{4,3,2,1,0:T(8,128)(2,1)}, bf16[1,1,16,32,320]{4,3,2,1,0:T(8,128)(2,1)S(1)}, u32[]{:S(2)}) copy-start(bf16[1,1,16,32,320]{4,3,2,1,0:T(8,128)(2,1)S(1)} %convert_element_type.18) | copy-start | bytes 983044
  15.5 11.9 %copy-start.3 = (f32[1,1,16,32,320]{4,3,2,1,0:T(8,128)S(1)}, f32[1,1,16,32,320]{4,3,2,1,0:T(8,128)}, u32[]{:S(2)}) copy-start(f32[1,1,16,32,320]{4,3,2,1,0:T(8,128)} %param.9) | copy-start | bytes 1966084
  36.5 3.1 %copy-start = (bf16[9,320,320]{2,1,0:T(8,128)(2,1)S(1)}, bf16[9,320,320]{2,1,0:T(8,128)(2,1)}, u32[]{:S(2)}) copy-start(bf16[9,320,320]{2,1,0:T(8,128)(2,1)} %all-gather.2.cloned.1.call-done) | copy-start | bytes 5529604
  38.1 3.0 %copy-start.18 = (bf16[1,1,16,32,320]{4,3,2,1,0:T(8,128)(2,1)S(1)}, bf16[1,1,16,32,320]{4,3,2,1,0:T(8,128)(2,1)}, u32[]{:S(2)}) copy-start(bf16[1,1,16,32,320]{4,3,2,1,0:T(8,128)(2,1)} %get-tuple-element.17) | copy-start | bytes 983044
  39.6 1.9 %copy-start.2 = (bf16[1,1,16,32,320]{4,3,2,1,0:T(8,128)(2,1)S(1)}, bf16[1,1,16,32,320]{4,3,2,1,0:T(8,128)(2,1)}, u32[]{:S(2)}) copy-start(bf16[1,1,16,32,320]{4,3,2,1,0:T(8,128)(2,1)} %copy-done.1) | copy-start | bytes 983044
  41.0 1.0 copy-start.17
  41.4 1.0 copy-start.16
  41.8 1.1 copy-start.15
  42.4 1.0 copy-start.20
  42.4 1.0 copy-start.22
  46.7 17.9 %collective-permute-start.1 = (bf16[1,1,16,32,320]{4,3,2,1,0:T(8,128)(2,1)}, bf16[1,1,16,32,320]{4,3,2,1,0:T(8,128)(2,1)}, u32[]{:S(2)}, u32[]{:S(2)}) collective-permute-start(bf16[1,1,16,32,320]{4,3,2,1,0:T(8,128)(2,1)} %bitcast.145), channel_id=1, source_target_pairs={{4,0},{8,4},{12,8},{16,12},{20,16},{24,20},{28,24},{5,1},{9,5},{13... | collective-permute-start | bytes 983048 | tf_op jit(solution)/shard_map/ppermute | solution.py:18
  48.0 21.6 %collective-permute-start = (bf16[1,1,16,32,320]{4,3,2,1,0:T(8,128)(2,1)}, bf16[1,1,16,32,320]{4,3,2,1,0:T(8,128)(2,1)}, u32[]{:S(2)}, u32[]{:S(2)}) collective-permute-start(bf16[1,1,16,32,320]{4,3,2,1,0:T(8,128)(2,1)} %bitcast.146), channel_id=1, source_target_pairs={{0,4},{4,8},{8,12},{12,16},{16,20},{20,24},{24,28},{1,5},{5,9},{9,... | collective-permute-start | bytes 983048 | tf_op jit(solution)/shard_map/ppermute | solution.py:16
  58.6 5.6 %copy-start.6 = (bf16[512,320]{0,1:T(8,128)(2,1)S(1)}, bf16[512,320]{0,1:T(8,128)(2,1)}, u32[]{:S(2)}) copy-start(bf16[512,320]{0,1:T(8,128)(2,1)} %get-tuple-element.22) | copy-start | bytes 983044
  72.2 3.0 %copy-start.10 = (bf16[1,1,16,32,320]{4,3,2,1,0:T(8,128)(2,1)S(1)}, bf16[1,1,16,32,320]{4,3,2,1,0:T(8,128)(2,1)}, u32[]{:S(2)}) copy-start(bf16[1,1,16,32,320]{4,3,2,1,0:T(8,128)(2,1)} %get-tuple-element.12) | copy-start | bytes 983044
  72.3 104.3 %all-reduce.4.cloned.1.call-start = ((), (), s32[]{:S(2)}) async-start(), calls=%async_computation.3 | async-start | bytes 737280 | tf_op jit(solution)/shard_map/psum | solution.py:79
  72.3 3.3 %copy-start.9 = (f32[512,320]{0,1:T(8,128)S(1)}, f32[512,320]{0,1:T(8,128)}, u32[]{:S(2)}) copy-start(f32[512,320]{0,1:T(8,128)} %copy.16) | copy-start | bytes 1966084
  72.3 3.3 %copy-start.14 = (bf16[1,1,16,32,320]{4,3,2,1,0:T(8,128)(2,1)S(1)}, bf16[1,1,16,32,320]{4,3,2,1,0:T(8,128)(2,1)}, u32[]{:S(2)}) copy-start(bf16[1,1,16,32,320]{4,3,2,1,0:T(8,128)(2,1)} %get-tuple-element.13) | copy-start | bytes 983044
  73.8 2.2 %copy-start.13 = (bf16[1,1,16,32,320]{4,3,2,1,0:T(8,128)(2,1)S(1)}, bf16[1,1,16,32,320]{4,3,2,1,0:T(8,128)(2,1)}, u32[]{:S(2)}) copy-start(bf16[1,1,16,32,320]{4,3,2,1,0:T(8,128)(2,1)} %get-tuple-element.7) | copy-start | bytes 983044
  75.6 1.0 copy-start.12
  76.0 1.0 copy-start.11
  76.4 1.1 copy-start.8
  76.4 1.2 copy-start.19
  77.6 3.5 %copy-start.7 = (bf16[512,320]{0,1:T(8,128)(2,1)S(1)}, bf16[512,320]{0,1:T(8,128)(2,1)}, u32[]{:S(2)}) copy-start(bf16[512,320]{0,1:T(8,128)(2,1)} %get-tuple-element.22) | copy-start | bytes 983044
  102.9 3.7 %copy-start.5 = (f32[1,1,16,32,320]{4,3,2,1,0:T(8,128)S(1)}, f32[1,1,16,32,320]{4,3,2,1,0:T(8,128)}, u32[]{:S(2)}) copy-start(f32[1,1,16,32,320]{4,3,2,1,0:T(8,128)} %param.5) | copy-start | bytes 1966084
Sparse Core Ops, SparseCore 0:
  9.6 26.8 all-gather.1
  72.4 29.1 reduce-scatter.1
  104.9 71.5 all-reduce.3
where the time goes:
time: 186 us; the launch traced here: 185 us
  waiting for transfers between devices  99 us (53%)
  matrix products  27.1 us (15%)
  local copies, waits for them, and re-layouts  15.7 us (8%)
  between operations  14.2 us (8%)
  starting transfers between devices  13.5 us (7%)
  blocking collectives  10.1 us (5%)
  other arithmetic  5.23 us (3%)
    psum x1, waiting for transfers between devices, on_device(): summed = lax.psum(local_grad, 'tm')  69 us
    reduce_scatter x1, waiting for transfers between devices, on_device(): owned = lax.psum_scatter(summed, 'clip', scatter_dimension=1, tiled=True)  20 us
    dot_general x12, matrix products, transpose_dot(): lax.dot_general(left, right, (((1,), (1,)), ((), ())), preferred_element_...  12.3 us
    ppermute x2, starting transfers between devices, padded_2(): lax.ppermute(tail, axis, [(i, (i + 1) % count) for i in range(ends)])  10.8 us
    all_gather x1, blocking collectives, on_device(): lax.all_gather(temporal_b, 'clip', axis=1, tiled=True)  10.1 us
    dot_general x9, matrix products, on_device(): jnp.dot(window, spatial_all[3 * shift_y + shift_x], preferred_element_typ...  7.74 us
    ppermute x2, waiting for transfers between devices, padded_2(): lax.ppermute(tail, axis, [(i, (i + 1) % count) for i in range(ends)])  4.81 us
    all_gather x1, waiting for transfers between devices, on_device(): lax.all_gather(spatial_w, 'clip', axis=1, tiled=True)  4.46 us
  transfers between devices with their start and end apart: 7, of which 5 were waited for; matrix products, arithmetic and copies ran while one was open for 23% of the time, Pallas kernels for 0%

commit v1 on v0

--- a/solution.py
+++ b/solution.py
@@ -3,6 +3,14 @@
 import jax.numpy as jnp
 from jax import lax
 from jax.sharding import PartitionSpec as P
+
+
+def added_up(x, name):
+    size, total = (lax.axis_size(name), x)
+    for stride in [1 << k for k in range(size.bit_length() - 1)]:
+        swap = [(i, i ^ stride) for i in range(size)]
+        total = total + lax.ppermute(total, name, swap)
+    return total
 
 
 def padded_2(cells, sides, width):
@@ -76,7 +84,7 @@
         grads.append(outer_dot(shifted_hid, cot_flat))
     local_grad = jnp.stack(grads)
     total_rows = row_count * lax.axis_size("tm") * lax.axis_size("clip")
-    summed = lax.psum(local_grad, "tm")
+    summed = added_up(local_grad, "tm")
     owned = lax.psum_scatter(summed, "clip", scatter_dimension=1, tiled=True)
     grad_temporal = owned * (1.0 / math.sqrt(total_rows))
     grad_spatial = (grad_hidden * sigmoid_s * (1.0 + spatial * (1.0 - sigmoid_s))).astype(

time: 186 us -> 254 us (1.37)
  waiting for transfers between devices: 99 us -> 160 us
  other arithmetic: 5.23 us -> 12.3 us
  starting transfers between devices: 13.5 us -> 18.4 us
  blocking collectives: 10.1 us -> 7.38 us
    psum x1 -> x0, waiting for transfers between devices: 69 us -> none  [on_device(): summed = lax.psum(local_grad, 'tm')]
    ppermute x0 -> x3, waiting for transfers between devices: none -> 67.1 us  [added_up(): total = total + lax.ppermute(total, name, swap)]
    reduce_scatter x1, waiting for transfers between devices: 20 us -> 55.2 us  [on_device(): owned = lax.psum_scatter(summed, 'clip', scatter_dimension=1, tiled=True)]
    all_gather x1, waiting for transfers between devices: 4.46 us -> 24.8 us  [on_device(): lax.all_gather(spatial_w, 'clip', axis=1, tiled=True)]
    add x0 -> x3, other arithmetic: none -> 7.45 us  [added_up(): total = total + lax.ppermute(total, name, swap)]
    ppermute x0 -> x3, starting transfers between devices: none -> 7.19 us  [added_up(): total = total + lax.ppermute(total, name, swap)]
    ppermute x2, waiting for transfers between devices: 0.01 us -> 5.22 us  [padded_2(): lax.ppermute(head, axis, [((i + 1) % count, i) for i in range(ends)])]
    all_gather x1, blocking collectives: 10.1 us -> 7.38 us  [on_device(): lax.all_gather(temporal_b, 'clip', axis=1, tiled=True)]
  transfers between devices with their start and end apart: 7 -> 9, of which waited for: 5 -> 7; matrix products, arithmetic and copies ran while one was open for 23% -> 14% of each run, Pallas kernels for 0% -> 0%
where the time goes in v1:
time: 254 us; the launch traced here: 253 us
  waiting for transfers between devices  160 us (63%)
  matrix products  25.1 us (10%)
  starting transfers between devices  18.4 us (7%)
  local copies, waits for them, and re-layouts  15.6 us (6%)
  between operations  14.5 us (6%)
  other arithmetic  12.3 us (5%)
  blocking collectives  7.38 us (3%)
    ppermute x3, waiting for transfers between devices, added_up(): total = total + lax.ppermute(total, name, swap)  67.1 us
    reduce_scatter x1, waiting for transfers between devices, on_device(): owned = lax.psum_scatter(summed, 'clip', scatter_dimension=1, tiled=True)  55.2 us
    all_gather x1, waiting for transfers between devices, on_device(): lax.all_gather(spatial_w, 'clip', axis=1, tiled=True)  24.8 us
    dot_general x12, matrix products, transpose_dot(): lax.dot_general(left, right, (((1,), (1,)), ((), ())), preferred_element_...  12.3 us
    ppermute x2, starting transfers between devices, padded_2(): lax.ppermute(tail, axis, [(i, (i + 1) % count) for i in range(ends)])  8.53 us
    add x3, other arithmetic, added_up(): total = total + lax.ppermute(total, name, swap)  7.45 us
    all_gather x1, blocking collectives, on_device(): lax.all_gather(temporal_b, 'clip', axis=1, tiled=True)  7.38 us
    ppermute x3, starting transfers between devices, added_up(): total = total + lax.ppermute(total, name, swap)  7.19 us
  transfers between devices with their start and end apart: 9, of which 7 were waited for; matrix products, arithmetic and copies ran while one was open for 14% of the time, Pallas kernels for 0%

profile of v1, /device:TPU:0, one launch (start us, length us, event | category | flops | bytes accessed | tf_op | source)
XLA Modules:
  0.0 253.3 jit_solution(659013013654978673)
XLA Ops:
  9.1 1.6 pad_slice_fusion.8
  10.7 24.8 %all-gather.2.cloned.1.call-done = bf16[9,320,320]{2,1,0:T(8,128)(2,1)} async-done(((bf16[9,80,320]{2,1,0:T(8,128)(2,1)}), bf16[9,320,320]{2,1,0:T(8,128)(2,1)}) %all-gather.2.cloned.1.call-update) | async-done | bytes 1843216 | tf_op jit(solution)/shard_map/all_gather | solution.py:52
  35.5 1.5 fusion.14
  37.0 1.5 convolution_add_fusion.14
  41.3 1.3 multiply_convert_fusion
  45.6 4.6 %collective-permute-start = (bf16[1,1,16,32,320]{4,3,2,1,0:T(8,128)(2,1)}, bf16[1,1,16,32,320]{4,3,2,1,0:T(8,128)(2,1)S(1)}, u32[]{:S(2)}, u32[]{:S(2)}) collective-permute-start(bf16[1,1,16,32,320]{4,3,2,1,0:T(8,128)(2,1)} %bitcast.146), channel_id=1, source_target_pairs={{0,4},{4,8},{8,12},{12,16},{16,20},{20,24},{24,28},{1,5},{5,9},{9,... | collective-permute-start | bytes 983048 | tf_op jit(solution)/shard_map/ppermute | solution.py:24
  50.2 1.4 convolution_bitcast_fusion.1
  51.6 5.2 %collective-permute-done.1 = bf16[1,1,16,32,320]{4,3,2,1,0:T(8,128)(2,1)S(1)} collective-permute-done((bf16[1,1,16,32,320]{4,3,2,1,0:T(8,128)(2,1)}, bf16[1,1,16,32,320]{4,3,2,1,0:T(8,128)(2,1)S(1)}, u32[]{:S(2)}, u32[]{:S(2)}) %collective-permute-start.1) | collective-permute-done | bytes 327712 | tf_op jit(solution)/shard_map/ppermute | solution.py:26
  56.8 1.5 convolution_bitcast_fusion
  58.4 6.9 %collective-permute-done = bf16[1,1,16,32,320]{4,3,2,1,0:T(8,128)(2,1)S(1)} collective-permute-done((bf16[1,1,16,32,320]{4,3,2,1,0:T(8,128)(2,1)}, bf16[1,1,16,32,320]{4,3,2,1,0:T(8,128)(2,1)S(1)}, u32[]{:S(2)}, u32[]{:S(2)}) %collective-permute-start) | collective-permute-done | bytes 327712 | tf_op jit(solution)/shard_map/ppermute | solution.py:24
  65.3 1.5 convolution_bitcast_fusion.2
  66.9 2.4 collective-permute-start.4
  69.4 32.5 %collective-permute-done.4 = f32[3,320,320]{2,1,0:T(8,128)S(1)} collective-permute-done((f32[3,320,320]{2,1,0:T(8,128)S(1)}, f32[3,320,320]{2,1,0:T(8,128)S(1)}, u32[]{:S(2)}, u32[]{:S(2)}) %collective-permute-start.4) | collective-permute-done | bytes 1228832 | tf_op jit(solution)/shard_map/ppermute | solution.py:12
  101.8 1.5 fusion.23
  103.4 1.9 collective-permute-start.5
  105.3 4.0 %collective-permute-start.3 = (bf16[1,1,16,32,320]{4,3,2,1,0:T(8,128)(2,1)}, bf16[1,1,16,32,320]{4,3,2,1,0:T(8,128)(2,1)}, u32[]{:S(2)}, u32[]{:S(2)}) collective-permute-start(bf16[1,1,16,32,320]{4,3,2,1,0:T(8,128)(2,1)} %convert_element_type.21), channel_id=1, source_target_pairs={{0,4},{4,8},{8,12},{12,16},{16,20},{20,24},{24,28},{1,5},{5,9},{9,... | collective-permute-start | bytes 983048 | tf_op jit(solution)/shard_map/ppermute | solution.py:24
  110.6 7.4 %all_gather.7 = bf16[3,320,320]{2,1,0:T(8,128)(2,1)S(1)} all-gather(bf16[3,80,320]{2,1,0:T(8,128)(2,1)S(1)} %convert_element_type.20), channel_id=1, replica_groups=mesh['tm'=8,'clip'=4] {'clip'}, dimensions={1}, use_global_device_ids=true | all-gather | bytes 768000 | tf_op jit(solution)/shard_map/all_gather | solution.py:53
  118.0 2.3 copy.16
  120.2 1.5 fusion.19
  121.7 1.4 fusion.21
  123.1 15.7 %collective-permute-done.5 = f32[3,320,320]{2,1,0:T(8,128)} collective-permute-done((f32[3,320,320]{2,1,0:T(8,128)}, f32[3,320,320]{2,1,0:T(8,128)}, u32[]{:S(2)}, u32[]{:S(2)}) %collective-permute-start.5) | collective-permute-done | bytes 1228832 | tf_op jit(solution)/shard_map/ppermute | solution.py:12
  138.8 2.8 %fusion.50 = f32[3,320,320]{2,1,0:T(8,128)} fusion(f32[3,320,320]{2,1,0:T(8,128)} %collective-permute-done.5, f32[3,320,320]{2,1,0:T(8,128)S(1)} %copy-done.2, f32[1,320,320]{2,1,0:T(8,128)S(1)} %copy-done.4, f32[1,320,320]{2,1,0:T(8,128)S(1)} %convolution_bitcast_fusion.1, f32[1,320,320]{2,1,0:T(8,128)S(1)} %copy-done.6), kind=kLoop, calls=%fused_computation.74 | loop fusion | flops 1228800 | bytes 4915200 | tf_op jit(solution)/shard_map/add | solution.py:12
  141.7 2.8 %collective-permute-start.6 = (f32[3,320,320]{2,1,0:T(8,128)}, f32[3,320,320]{2,1,0:T(8,128)}, u32[]{:S(2)}, u32[]{:S(2)}) collective-permute-start(f32[3,320,320]{2,1,0:T(8,128)} %fusion.50), channel_id=1, source_target_pairs={{0,16},{4,20},{8,24},{12,28},{16,0},{20,4},{24,8},{28,12},{1,17},{... | collective-permute-start | bytes 3686408 | tf_op jit(solution)/shard_map/ppermute | solution.py:12
  144.5 1.5 fusion.9
  146.9 4.8 %pad_slice_fusion.4 = (bf16[1,1,16,32,320]{4,3,2,1,0:T(8,128)(2,1)}, bf16[1,1,16,32,320]{4,3,2,1,0:T(8,128)(2,1)}, bf16[1,1,16,32,320]{4,3,2,1,0:T(8,128)(2,1)},...) fusion(bf16[1,1,16,32,320]{4,3,2,1,0:T(8,128)(2,1)} %bitcast.130), kind=kLoop, calls=%fused_computation.35 | loop fusion | bytes 2949120 | tf_op jit(solution)/shard_map/slice | solution.py:100
  155.3 18.9 %collective-permute-done.6 = f32[3,320,320]{2,1,0:T(8,128)} collective-permute-done((f32[3,320,320]{2,1,0:T(8,128)}, f32[3,320,320]{2,1,0:T(8,128)}, u32[]{:S(2)}, u32[]{:S(2)}) %collective-permute-start.6) | collective-permute-done | bytes 1228832 | tf_op jit(solution)/shard_map/ppermute | solution.py:12
  174.2 3.1 %add.123 = f32[3,320,320]{2,1,0:T(8,128)} add(f32[3,320,320]{2,1,0:T(8,128)} %fusion.50, f32[3,320,320]{2,1,0:T(8,128)} %collective-permute-done.6) | non-fusion elementwise | flops 307200 | bytes 3686400 | tf_op jit(solution)/shard_map/add | solution.py:12
  177.8 1.6 convolution_add_fusion.4
  182.6 2.3 copy.17
  187.1 1.3 copy.14
  189.5 55.2 %reduce-scatter.2.cloned.1.call-done = f32[3,80,320]{2,1,0:T(8,128)} async-done(((f32[3,320,320]{2,1,0:T(8,128)}), f32[3,80,320]{2,1,0:T(8,128)}) %reduce-scatter.2.cloned.1.call-update) | async-done | bytes 307216 | tf_op jit(solution)/shard_map/reduce_scatter | solution.py:88
  244.7 1.7 broadcast_multiply_fusion
  (94 shorter events, 20.4 us)
Async XLA Ops:
  7.2 28.3 %all-gather.2.cloned.1.call-start = ((), (), s32[]{:S(2)}) async-start(), calls=%async_computation.1 | async-start | bytes 2764800 | tf_op jit(solution)/shard_map/all_gather | solution.py:52
  7.9 236.8 %reduce-scatter.2.cloned.1.call-start = ((), (), s32[]{:S(2)}) async-start(), calls=%async_computation.2 | async-start | bytes 1843200 | tf_op jit(solution)/shard_map/reduce_scatter | solution.py:88
  35.5 3.0 %copy-start = (bf16[9,320,320]{2,1,0:T(8,128)(2,1)S(1)}, bf16[9,320,320]{2,1,0:T(8,128)(2,1)}, u32[]{:S(2)}) copy-start(bf16[9,320,320]{2,1,0:T(8,128)(2,1)} %all-gather.2.cloned.1.call-done) | copy-start | bytes 5529604
  35.5 3.0 %copy-start.20 = (bf16[1,1,16,32,320]{4,3,2,1,0:T(8,128)(2,1)S(1)}, bf16[1,1,16,32,320]{4,3,2,1,0:T(8,128)(2,1)}, u32[]{:S(2)}) copy-start(bf16[1,1,16,32,320]{4,3,2,1,0:T(8,128)(2,1)} %get-tuple-element.16) | copy-start | bytes 983044
  37.0 1.9 copy-start.19
  41.3 3.5 %copy-start.7 = (f32[1,1,16,32,320]{4,3,2,1,0:T(8,128)S(1)}, f32[1,1,16,32,320]{4,3,2,1,0:T(8,128)}, u32[]{:S(2)}) copy-start(f32[1,1,16,32,320]{4,3,2,1,0:T(8,128)} %param.9) | copy-start | bytes 1966084
  42.6 7.6 %copy-start.9 = (bf16[512,320]{0,1:T(8,128)(2,1)}, bf16[512,320]{0,1:T(8,128)(2,1)S(1)}, u32[]{:S(2)}) copy-start(bf16[512,320]{0,1:T(8,128)(2,1)S(1)} %get-tuple-element.22) | copy-start | bytes 983044
  43.5 13.3 %collective-permute-start.1 = (bf16[1,1,16,32,320]{4,3,2,1,0:T(8,128)(2,1)}, bf16[1,1,16,32,320]{4,3,2,1,0:T(8,128)(2,1)S(1)}, u32[]{:S(2)}, u32[]{:S(2)}) collective-permute-start(bf16[1,1,16,32,320]{4,3,2,1,0:T(8,128)(2,1)} %bitcast.145), channel_id=1, source_target_pairs={{4,0},{8,4},{12,8},{16,12},{20,16},{24,20},{28,24},{5,1},{9,5},{13... | collective-permute-start | bytes 983048 | tf_op jit(solution)/shard_map/ppermute | solution.py:26
  45.6 19.6 %collective-permute-start = (bf16[1,1,16,32,320]{4,3,2,1,0:T(8,128)(2,1)}, bf16[1,1,16,32,320]{4,3,2,1,0:T(8,128)(2,1)S(1)}, u32[]{:S(2)}, u32[]{:S(2)}) collective-permute-start(bf16[1,1,16,32,320]{4,3,2,1,0:T(8,128)(2,1)} %bitcast.146), channel_id=1, source_target_pairs={{0,4},{4,8},{8,12},{12,16},{16,20},{20,24},{24,28},{1,5},{5,9},{9,... | collective-permute-start | bytes 983048 | tf_op jit(solution)/shard_map/ppermute | solution.py:24
  56.8 8.4 %copy-start.26 = (bf16[1,1,16,32,320]{4,3,2,1,0:T(8,128)(2,1)}, bf16[1,1,16,32,320]{4,3,2,1,0:T(8,128)(2,1)S(1)}, u32[]{:S(2)}) copy-start(bf16[1,1,16,32,320]{4,3,2,1,0:T(8,128)(2,1)S(1)} %collective-permute-done.1) | copy-start | bytes 983044
  58.4 43.5 %copy-start.3 = (f32[1,320,320]{2,1,0:T(8,128)}, f32[1,320,320]{2,1,0:T(8,128)S(1)}, u32[]{:S(2)}) copy-start(f32[1,320,320]{2,1,0:T(8,128)S(1)} %convolution_bitcast_fusion) | copy-start | bytes 1228804
  65.3 1.6 copy-start.23
  66.8 36.6 %copy-start.5 = (f32[1,320,320]{2,1,0:T(8,128)}, f32[1,320,320]{2,1,0:T(8,128)S(1)}, u32[]{:S(2)}) copy-start(f32[1,320,320]{2,1,0:T(8,128)S(1)} %convolution_bitcast_fusion.2) | copy-start | bytes 1228804
  66.9 43.6 %copy-start.28 = (f32[3,80,320]{2,1,0:T(8,128)S(1)}, f32[3,80,320]{2,1,0:T(8,128)}, u32[]{:S(2)}) copy-start(f32[3,80,320]{2,1,0:T(8,128)} %param.8) | copy-start | bytes 921604
  66.9 34.9 %collective-permute-start.4 = (f32[3,320,320]{2,1,0:T(8,128)S(1)}, f32[3,320,320]{2,1,0:T(8,128)S(1)}, u32[]{:S(2)}, u32[]{:S(2)}) collective-permute-start(f32[3,320,320]{2,1,0:T(8,128)S(1)} %pad_maximum_fusion), channel_id=1, source_target_pairs={{0,4},{4,0},{8,12},{12,8},{16,20},{20,16},{24,28},{28,24},{1,5},{5... | collective-permute-start | bytes 3686408 | tf_op jit(solution)/shard_map/ppermute | solution.py:12
  101.8 8.7 %copy-start.1 = (f32[3,320,320]{2,1,0:T(8,128)}, f32[3,320,320]{2,1,0:T(8,128)S(1)}, u32[]{:S(2)}) copy-start(f32[3,320,320]{2,1,0:T(8,128)S(1)} %collective-permute-done.4) | copy-start | bytes 3686404
  103.4 35.5 %collective-permute-start.5 = (f32[3,320,320]{2,1,0:T(8,128)}, f32[3,320,320]{2,1,0:T(8,128)}, u32[]{:S(2)}, u32[]{:S(2)}) collective-permute-start(f32[3,320,320]{2,1,0:T(8,128)} %fusion.23), channel_id=1, source_target_pairs={{0,8},{4,12},{8,0},{12,4},{16,24},{20,28},{24,16},{28,20},{1,9},{5... | collective-permute-start | bytes 3686408 | tf_op jit(solution)/shard_map/ppermute | solution.py:12
  105.3 16.5 %collective-permute-start.3 = (bf16[1,1,16,32,320]{4,3,2,1,0:T(8,128)(2,1)}, bf16[1,1,16,32,320]{4,3,2,1,0:T(8,128)(2,1)}, u32[]{:S(2)}, u32[]{:S(2)}) collective-permute-start(bf16[1,1,16,32,320]{4,3,2,1,0:T(8,128)(2,1)} %convert_element_type.21), channel_id=1, source_target_pairs={{0,4},{4,8},{8,12},{12,16},{16,20},{20,24},{24,28},{1,5},{5,9},{9,... | collective-permute-start | bytes 983048 | tf_op jit(solution)/shard_map/ppermute | solution.py:24
  109.2 35.3 %collective-permute-start.2 = (bf16[1,1,16,32,320]{4,3,2,1,0:T(8,128)(2,1)}, bf16[1,1,16,32,320]{4,3,2,1,0:T(8,128)(2,1)}, u32[]{:S(2)}, u32[]{:S(2)}) collective-permute-start(bf16[1,1,16,32,320]{4,3,2,1,0:T(8,128)(2,1)} %convert_element_type.21), channel_id=1, source_target_pairs={{4,0},{8,4},{12,8},{16,12},{20,16},{24,20},{28,24},{5,1},{9,5},{13... | collective-permute-start | bytes 983048 | tf_op jit(solution)/shard_map/ppermute | solution.py:26
  120.2 18.6 %copy-start.2 = (f32[3,320,320]{2,1,0:T(8,128)S(1)}, f32[3,320,320]{2,1,0:T(8,128)}, u32[]{:S(2)}) copy-start(f32[3,320,320]{2,1,0:T(8,128)} %copy-done.1) | copy-start | bytes 3686404
  120.2 18.6 %copy-start.4 = (f32[1,320,320]{2,1,0:T(8,128)S(1)}, f32[1,320,320]{2,1,0:T(8,128)}, u32[]{:S(2)}) copy-start(f32[1,320,320]{2,1,0:T(8,128)} %copy-done.3) | copy-start | bytes 1228804
  120.2 18.6 %copy-start.6 = (f32[1,320,320]{2,1,0:T(8,128)S(1)}, f32[1,320,320]{2,1,0:T(8,128)}, u32[]{:S(2)}) copy-start(f32[1,320,320]{2,1,0:T(8,128)} %copy-done.5) | copy-start | bytes 1228804
  123.1 21.4 %copy-start.30 = (f32[512,320]{0,1:T(8,128)S(1)}, f32[512,320]{0,1:T(8,128)}, u32[]{:S(2)}) copy-start(f32[512,320]{0,1:T(8,128)} %get-tuple-element.23) | copy-start | bytes 1966084
  141.7 32.6 %collective-permute-start.6 = (f32[3,320,320]{2,1,0:T(8,128)}, f32[3,320,320]{2,1,0:T(8,128)}, u32[]{:S(2)}, u32[]{:S(2)}) collective-permute-start(f32[3,320,320]{2,1,0:T(8,128)} %fusion.50), channel_id=1, source_target_pairs={{0,16},{4,20},{8,24},{12,28},{16,0},{20,4},{24,8},{28,12},{1,17},{... | collective-permute-start | bytes 3686408 | tf_op jit(solution)/shard_map/ppermute | solution.py:12
  177.4 2.0 copy-start.16
  177.8 2.1 copy-start.15
  179.8 1.3 copy-start.12
  179.8 1.5 copy-start.13
  179.8 1.6 copy-start.22
  181.4 3.5 %copy-start.10 = (bf16[512,320]{0,1:T(8,128)(2,1)S(1)}, bf16[512,320]{0,1:T(8,128)(2,1)}, u32[]{:S(2)}) copy-start(bf16[512,320]{0,1:T(8,128)(2,1)} %copy-done.9) | copy-start | bytes 983044
  182.6 2.7 %copy-start.27 = (bf16[1,1,16,32,320]{4,3,2,1,0:T(8,128)(2,1)S(1)}, bf16[1,1,16,32,320]{4,3,2,1,0:T(8,128)(2,1)}, u32[]{:S(2)}) copy-start(bf16[1,1,16,32,320]{4,3,2,1,0:T(8,128)(2,1)} %copy-done.26) | copy-start | bytes 983044
  185.7 2.8 %copy-start.8 = (f32[1,1,16,32,320]{4,3,2,1,0:T(8,128)S(1)}, f32[1,1,16,32,320]{4,3,2,1,0:T(8,128)}, u32[]{:S(2)}) copy-start(f32[1,1,16,32,320]{4,3,2,1,0:T(8,128)} %param.5) | copy-start | bytes 1966084
  (8 other events, 8.1 us)
Sparse Core Ops, SparseCore 0:
  9.5 25.9 all-gather.1
  177.5 67.1 reduce-scatter.1
